TPU v7x, 32 devices: a whole 2x2x4 slice. The times are simulated.
32 devices in a mesh: groups: 2 (over y), seq: 4 (over z), head: 4 (over x, core).
Axes of the slice: x: 2, y: 2, z: 4, core: 2. Of those that a mesh axis runs over, the one named last changes fastest.
Arguments:
- queries: bfloat16 [4096, 2048], P(('groups', 'seq'), 'head'), parts along dimension 0, may hold values from -8 to 8
- keys: bfloat16 [4096, 2048], P(('groups', 'seq'), 'head'), parts along dimension 0, may hold values from -8 to 8
- values: bfloat16 [4096, 2048], P(('groups', 'seq'), 'head'), parts along dimension 0, may hold values from -12 to 12
- w_out: bfloat16 [2048, 2048], replicated, may hold values from -0.125 to 0.125
Outputs:
- projected: bfloat16 [4096, 2048], P(('groups', 'seq', 'head')), parts along dimension 0
There are 2 independent parts, one for each index of `groups`. A program takes and returns all parts, laid end to end along the dimension named above; an argument that names none is the same for every part. Nothing has to cross between parts.
All inputs are finite; a program needn't handle non-finite values.
Results may differ from a plain program's by a relative error of at most 0.005.
Values may be sent and summed in bfloat16 or wider, within the bound.
A program may use at most 128 MiB of HBM per device.

v0:
```python
import math

import jax
import jax.numpy as jnp
from jax import lax
from jax.sharding import PartitionSpec as P

HD = 128
WINDOW = 2048


def shifted(value, axis, steps):
    count = lax.axis_size(axis)
    first, last = (max(0, -steps), min(count, count - steps))
    return lax.ppermute(value, axis, [(source, source + steps) for source in range(first, last)])


def per_device(queries, keys, values, w_out):
    length_dev, width = queries.shape
    heads_dev = width // HD
    block_rows = min(512, length_dev)
    block_count = length_dev // block_rows
    highest = lax.Precision.HIGHEST
    seq_index = lax.axis_index("seq")
    q_blocks = queries.reshape(block_count, block_rows, heads_dev, HD)
    k_blocks = keys.reshape(block_count, block_rows, heads_dev, HD)
    v_blocks = values.reshape(block_count, block_rows, heads_dev, HD)
    block_states = jnp.einsum(
        "bkhd,bkhe->bhde", k_blocks, v_blocks, preferred_element_type=jnp.float32
    )
    own_state = jnp.sum(block_states, axis=0)
    earlier = jnp.cumsum(block_states, axis=0) - block_states
    piece = lax.all_gather(own_state[None], "seq", axis=0, tiled=True)
    order = jnp.arange(piece.shape[0], dtype=jnp.int32)
    keep = order < seq_index
    prefix = jnp.sum(jnp.where(keep[:, None, None, None], piece, 0.0), axis=0)
    causal = jnp.arange(block_rows)[:, None] >= jnp.arange(block_rows)[None, :]
    local_scores = jnp.einsum(
        "bqhd,bkhd->bhqk", q_blocks, k_blocks, preferred_element_type=jnp.float32
    )
    local_scores = jnp.where(causal, local_scores, 0.0)
    intra = jnp.einsum(
        "bhqk,bkhe->bqhe", local_scores, v_blocks.astype(jnp.float32), precision=highest
    )
    state_before = prefix[None] + earlier
    inter = jnp.einsum(
        "bqhd,bhde->bqhe", q_blocks.astype(jnp.float32), state_before, precision=highest
    )
    linear = (intra + inter).reshape(length_dev, heads_dev, HD)
    normed = linear / jnp.sqrt(jnp.mean(linear * linear, axis=-1, keepdims=True) + 1e-06)
    reach = min(WINDOW // length_dev, lax.axis_size("seq") - 1)
    received = [shifted((keys, values), "seq", distance) for distance in range(1, reach + 1)]
    pad_rows = WINDOW - reach * length_dev
    filler = jnp.zeros((pad_rows, width), keys.dtype)
    wide_keys = jnp.concatenate([filler] + [pair[0] for pair in reversed(received)] + [keys], 0)
    wide_values = jnp.concatenate([filler] + [pair[1] for pair in reversed(received)] + [values], 0)
    wide_keys = wide_keys.reshape(-1, heads_dev, HD)
    wide_values = wide_values.reshape(-1, heads_dev, HD)
    scale = 1.0 / math.sqrt(HD)
    span = WINDOW + block_rows
    query_pos = jnp.arange(block_rows, dtype=jnp.int32)[:, None]
    key_pos = jnp.arange(span, dtype=jnp.int32)[None, :]
    band = (key_pos > query_pos) & (key_pos <= query_pos + WINDOW)
    rows_q = queries.reshape(block_rows, heads_dev, HD)
    anchor = seq_index * length_dev + 0 - WINDOW
    valid = band & (anchor + key_pos >= 0)
    scores = (
        jnp.einsum("qhd,khd->hqk", rows_q, wide_keys, preferred_element_type=jnp.float32) * scale
    )
    scores = jnp.where(valid[None], scores, -1e30)
    top = jnp.max(scores, axis=-1, keepdims=True)
    expo = jnp.where(valid[None], jnp.exp(scores - top), 0.0)
    total = jnp.sum(expo, axis=-1)
    weights = expo.astype(jnp.bfloat16)
    summed = jnp.einsum("hqk,khe->qhe", weights, wide_values, preferred_element_type=jnp.float32)
    pieces = summed / jnp.transpose(total)[:, :, None]
    mixed = (normed + pieces).astype(jnp.bfloat16).reshape(length_dev, width)
    head_count = lax.axis_size("head")
    share = length_dev // head_count
    grouped = mixed.reshape(head_count, share, width)
    return jnp.dot(
        lax.all_to_all(grouped, "head", split_axis=0, concat_axis=2, tiled=True)[0],
        w_out,
        preferred_element_type=jnp.float32,
    ).astype(jnp.bfloat16)


def solution(mesh):
    return jax.shard_map(
        per_device,
        mesh=mesh,
        in_specs=(
            P(("groups", "seq"), "head"),
            P(("groups", "seq"), "head"),
            P(("groups", "seq"), "head"),
            P(),
        ),
        out_specs=P(("groups", "seq", "head"), None),
        check_vma=False,
    )
```

profile of v0, /device:TPU:16, one launch (start us, length us, event | category | flops | bytes accessed | tf_op | source)
XLA Modules:
  0.0 174.5 jit_solution(8869428141898482623)
XLA Ops:
  6.5 1.3 copy.52
  7.9 1.5 collective-permute-start.3
  9.3 1.3 collective-permute-start.4
  10.6 3.3 %collective-permute-start.5 = (bf16[512,512]{0,1:T(8,128)(2,1)S(1)}, bf16[512,512]{0,1:T(8,128)(2,1)}, u32[]{:S(2)}, u32[]{:S(2)}) collective-permute-start(bf16[512,512]{0,1:T(8,128)(2,1)S(1)} %copy.52), channel_id=1, source_target_pairs={{0,4},{4,8},{8,12},{1,5},{5,9},{9,13},{2,6},{6,10},{10,14},{3,7},{... | collective-permute-start | bytes 1572872 | tf_op jit(solution)/shard_map/ppermute | solution.py:15
  13.9 1.3 copy.37
  15.2 1.5 collective-permute-start
  16.7 1.3 collective-permute-start.1
  18.0 2.0 %fusion.37 = f32[4,128,128]{2,1,0:T(8,128)} fusion(bf16[512,4,128]{0,2,1:T(8,128)(2,1)S(1)} %bitcast.96, bf16[512,512]{1,0:T(8,128)(2,1)} %param.6), kind=kOutput, calls=%fused_computation.30 | convolution fusion | flops 67108864 | bytes 1310720 | tf_op jit(solution)/shard_map/bkhd,bkhe->bhde/dot_general | solution.py:28
  20.1 1.9 %fusion.8 = pred[512,2560]{0,1:T(8,128)(4,1)S(1)} fusion(s32[512]{0:T(512)S(1)} %iota_add_fusion, pred[2560]{0:T(1024)(128)(4,1)S(1)} %add_compare_fusion), kind=kLoop, calls=%fused_computation.12 | loop fusion | flops 5242880 | bytes 1315328 | tf_op jit(solution)/shard_map/and | solution.py:66
  22.0 2.8 %fusion.46 = f32[4,512,512]{2,1,0:T(8,128)} fusion(bf16[512,4,128]{0,2,1:T(8,128)(2,1)S(1)} %bitcast.97, bf16[512,512]{1,0:T(8,128)(2,1)S(1)} %copy-done), kind=kOutput, calls=%fused_computation.37 | convolution fusion | flops 268435456 | bytes 5242880 | tf_op jit(solution)/shard_map/bqhd,bkhd->bhqk/dot_general | solution.py:38
  24.9 5.3 %collective-permute-start.2 = (bf16[512,512]{0,1:T(8,128)(2,1)S(1)}, bf16[512,512]{0,1:T(8,128)(2,1)S(1)}, u32[]{:S(2)}, u32[]{:S(2)}) collective-permute-start(bf16[512,512]{0,1:T(8,128)(2,1)S(1)} %copy.37), channel_id=1, source_target_pairs={{0,4},{4,8},{8,12},{1,5},{5,9},{9,13},{2,6},{6,10},{10,14},{3,7},{... | collective-permute-start | bytes 1572872 | tf_op jit(solution)/shard_map/ppermute | solution.py:15
  30.2 1.1 constant_dynamic-update-slice_fusion.7
  31.3 10.9 %collective-permute-done.4 = bf16[512,512]{0,1:T(8,128)(2,1)} collective-permute-done((bf16[512,512]{0,1:T(8,128)(2,1)S(1)}, bf16[512,512]{0,1:T(8,128)(2,1)}, u32[]{:S(2)}, u32[]{:S(2)}) %collective-permute-start.4) | collective-permute-done | bytes 524320 | tf_op jit(solution)/shard_map/ppermute | solution.py:15
  43.3 55.3 %collective-permute-done.5 = bf16[512,512]{0,1:T(8,128)(2,1)} collective-permute-done((bf16[512,512]{0,1:T(8,128)(2,1)S(1)}, bf16[512,512]{0,1:T(8,128)(2,1)}, u32[]{:S(2)}, u32[]{:S(2)}) %collective-permute-start.5) | collective-permute-done | bytes 524320 | tf_op jit(solution)/shard_map/ppermute | solution.py:15
  99.7 1.5 constant_dynamic-update-slice_fusion.3
  101.2 1.1 constant_dynamic-update-slice_fusion.2
  102.3 18.6 %collective-permute-done.2 = bf16[512,512]{0,1:T(8,128)(2,1)S(1)} collective-permute-done((bf16[512,512]{0,1:T(8,128)(2,1)S(1)}, bf16[512,512]{0,1:T(8,128)(2,1)S(1)}, u32[]{:S(2)}, u32[]{:S(2)}) %collective-permute-start.2) | collective-permute-done | bytes 524320 | tf_op jit(solution)/shard_map/ppermute | solution.py:15
  121.0 1.4 copy-done.3
  122.4 15.3 %fusion.63 = (f32[4,512]{1,0:T(4,128)S(1)}, bf16[4,512,2560]{1,2,0:T(8,128)(2,1)}) fusion(pred[512,2560]{0,1:T(8,128)(4,1)S(1)} %fusion.8, bf16[2560,4,128]{0,2,1:T(8,128)(2,1)} %bitcast.101, bf16[512,512]{1,0:T(8,128)(2,1)S(1)} %copy-done), kind=kOutput, calls=%fused_computation.64 | convolution fusion | flops 1373637120 | bytes 14950400 | tf_op jit(solution)/shard_map/sub | solution.py:72
  137.7 1.4 select_reduce_fusion
  139.8 5.2 %multiply_reduce_fusion = (f32[512,4]{0,1:T(4,128)S(1)}, f32[512,4,128]{0,2,1:T(8,128)S(1)}) fusion(f32[4,128,512]{2,1,0:T(8,128)S(1)} %fusion.44, f32[4,512,512]{2,1,0:T(8,128)} %fusion.46, pred[512,512]{1,0:T(8,128)(4,1)S(1)} %iota_compare_fusion.2, bf16[512,512]{1,0:T(8,128)(2,1)S(1)} %copy-done.1), kind=kOutput, calls=%fused_computation.26 | convolution fusion | flops 1612445696 | bytes 7086080 | tf_op jit(solution)/shard_map/bhqk,bkhe->bqhe/dot_general | solution.py:42
  145.0 5.6 %fusion.33 = bf16[512,4,128]{0,2,1:T(8,128)(2,1)S(1)} fusion(bf16[2560,4,128]{0,2,1:T(8,128)(2,1)S(1)} %bitcast.100, bf16[4,512,2560]{1,2,0:T(8,128)(2,1)} %get-tuple-element.6, f32[512,4,128]{0,2,1:T(8,128)S(1)} %get-tuple-element.8, f32[512,4]{0,1:T(4,128)S(1)} %bitcast.102, f32[512,4]{0,1:T(4,128)S(1)} %add_sqrt_fusion), kind=kOutput, calls=%fused_computation.25 | convolution fusion | flops 1343225856 | bytes 14696448 | tf_op jit(solution)/shard_map/hqk,khe->qhe/dot_general | solution.py:75
  150.8 11.4 %all_to_all.15 = bf16[4,128,512]{1,2,0:T(8,128)(2,1)S(1)} all-to-all(bf16[4,128,512]{1,2,0:T(8,128)(2,1)S(1)} %copy.48), channel_id=1, replica_groups=mesh['groups'=2,'seq'=4,'head'=4] {'head'}, dimensions={0} | all-to-all | bytes 1048576 | tf_op jit(solution)/shard_map/all_to_all | solution.py:82
  162.2 5.5 %convolution_convert_fusion = bf16[128,2048]{1,0:T(8,128)(2,1)} fusion(bf16[128,2048]{0,1:T(8,128)(2,1)S(1)} %bitcast.98, bf16[2048,2048]{1,0:T(8,128)(2,1)} %param.7), kind=kOutput, calls=%fused_computation.15 | convolution fusion | flops 1074003968 | bytes 9437184 | tf_op jit(solution)/shard_map/dot_general | solution.py:81
  (32 shorter events, 3.3 us)
Async XLA Ops:
  6.5 15.4 %copy-start = (bf16[512,512]{1,0:T(8,128)(2,1)S(1)}, bf16[512,512]{1,0:T(8,128)(2,1)}, u32[]{:S(2)}) copy-start(bf16[512,512]{1,0:T(8,128)(2,1)} %param.4) | copy-start | bytes 1572868
  6.5 131.2 %all-gather.3.cloned.1.call-start = ((), (), s32[]{:S(2)}) async-start(), calls=%async_computation.1 | async-start | bytes 1310720 | tf_op jit(solution)/shard_map/all_gather | solution.py:33
  7.9 17.1 %collective-permute-start.3 = (bf16[512,512]{0,1:T(8,128)(2,1)S(1)}, bf16[512,512]{0,1:T(8,128)(2,1)}, u32[]{:S(2)}, u32[]{:S(2)}) collective-permute-start(bf16[512,512]{0,1:T(8,128)(2,1)S(1)} %copy.52), channel_id=1, source_target_pairs={{0,12},{1,13},{2,14},{3,15},{16,28},{17,29},{18,30},{19,31}} | collective-permute-start | bytes 1572872 | tf_op jit(solution)/shard_map/ppermute | solution.py:15
  9.3 32.9 %collective-permute-start.4 = (bf16[512,512]{0,1:T(8,128)(2,1)S(1)}, bf16[512,512]{0,1:T(8,128)(2,1)}, u32[]{:S(2)}, u32[]{:S(2)}) collective-permute-start(bf16[512,512]{0,1:T(8,128)(2,1)S(1)} %copy.52), channel_id=1, source_target_pairs={{0,8},{4,12},{1,9},{5,13},{2,10},{6,14},{3,11},{7,15},{16,24},{20,... | collective-permute-start | bytes 1572872 | tf_op jit(solution)/shard_map/ppermute | solution.py:15
  10.6 88.0 %collective-permute-start.5 = (bf16[512,512]{0,1:T(8,128)(2,1)S(1)}, bf16[512,512]{0,1:T(8,128)(2,1)}, u32[]{:S(2)}, u32[]{:S(2)}) collective-permute-start(bf16[512,512]{0,1:T(8,128)(2,1)S(1)} %copy.52), channel_id=1, source_target_pairs={{0,4},{4,8},{8,12},{1,5},{5,9},{9,13},{2,6},{6,10},{10,14},{3,7},{... | collective-permute-start | bytes 1572872 | tf_op jit(solution)/shard_map/ppermute | solution.py:15
  15.2 84.5 %collective-permute-start = (bf16[512,512]{0,1:T(8,128)(2,1)S(1)}, bf16[512,512]{0,1:T(8,128)(2,1)}, u32[]{:S(2)}, u32[]{:S(2)}) collective-permute-start(bf16[512,512]{0,1:T(8,128)(2,1)S(1)} %copy.37), channel_id=1, source_target_pairs={{0,12},{1,13},{2,14},{3,15},{16,28},{17,29},{18,30},{19,31}} | collective-permute-start | bytes 1572872 | tf_op jit(solution)/shard_map/ppermute | solution.py:15
  16.7 84.5 %collective-permute-start.1 = (bf16[512,512]{0,1:T(8,128)(2,1)S(1)}, bf16[512,512]{0,1:T(8,128)(2,1)}, u32[]{:S(2)}, u32[]{:S(2)}) collective-permute-start(bf16[512,512]{0,1:T(8,128)(2,1)S(1)} %copy.37), channel_id=1, source_target_pairs={{0,8},{4,12},{1,9},{5,13},{2,10},{6,14},{3,11},{7,15},{16,24},{20,... | collective-permute-start | bytes 1572872 | tf_op jit(solution)/shard_map/ppermute | solution.py:15
  24.9 95.9 %collective-permute-start.2 = (bf16[512,512]{0,1:T(8,128)(2,1)S(1)}, bf16[512,512]{0,1:T(8,128)(2,1)S(1)}, u32[]{:S(2)}, u32[]{:S(2)}) collective-permute-start(bf16[512,512]{0,1:T(8,128)(2,1)S(1)} %copy.37), channel_id=1, source_target_pairs={{0,4},{4,8},{8,12},{1,5},{5,9},{9,13},{2,6},{6,10},{10,14},{3,7},{... | collective-permute-start | bytes 1572872 | tf_op jit(solution)/shard_map/ppermute | solution.py:15
  99.7 21.2 %copy-start.5 = (bf16[2560,512]{0,1:T(8,128)(2,1)}, bf16[2560,512]{0,1:T(8,128)(2,1)S(1)}, u32[]{:S(2)}) copy-start(bf16[2560,512]{0,1:T(8,128)(2,1)S(1)} %constant_dynamic-update-slice_fusion.4) | copy-start | bytes 7864324
  121.0 1.5 copy-start.3
  122.4 16.8 %copy-start.2 = (f32[4,128,128]{2,1,0:T(8,128)S(1)}, f32[4,128,128]{2,1,0:T(8,128)}, u32[]{:S(2)}) copy-start(f32[4,128,128]{2,1,0:T(8,128)} %fusion.37) | copy-start | bytes 786436
  137.7 2.1 %copy-start.1 = (bf16[512,512]{1,0:T(8,128)(2,1)S(1)}, bf16[512,512]{1,0:T(8,128)(2,1)}, u32[]{:S(2)}) copy-start(bf16[512,512]{1,0:T(8,128)(2,1)} %param.6) | copy-start | bytes 1572868
  139.8 5.2 %copy-start.4 = (bf16[2560,512]{0,1:T(8,128)(2,1)S(1)}, bf16[2560,512]{0,1:T(8,128)(2,1)}, u32[]{:S(2)}) copy-start(bf16[2560,512]{0,1:T(8,128)(2,1)} %copy-done.3) | copy-start | bytes 7864324
Sparse Core Ops, SparseCore 0:
  20.2 60.3 all-gather.2
where the time goes:
time: 175 us; the launch traced here: 174 us
  waiting for transfers between devices  84.8 us (48%)
  matrix products  36.9 us (21%)
  starting transfers between devices  14.2 us (8%)
  between operations  13.7 us (8%)
  blocking collectives  11.4 us (7%)
  local copies, waits for them, and re-layouts  10.2 us (6%)
  other arithmetic  3.42 us (2%)
    ppermute x6, waiting for transfers between devices, shifted(): lax.ppermute(value, axis, [(source, source + steps) for source in range(f...  84.7 us
    sub x1, matrix products, per_device(): expo = jnp.where(valid[None], jnp.exp(scores - top), 0.0)  15.3 us
    ppermute x6, starting transfers between devices, shifted(): lax.ppermute(value, axis, [(source, source + steps) for source in range(f...  14.2 us
    all_to_all x1, blocking collectives, per_device(): lax.all_to_all(grouped, 'head', split_axis=0, concat_axis=2, tiled=True)[0]  11.4 us
    unnamed x21, local copies, waits for them, and re-layouts  8.63 us
    dot_general x1, matrix products, per_device(): jnp.einsum('hqk,khe->qhe', weights, wide_values, preferred_element_type=j...  5.56 us
    dot_general x1, matrix products, per_device(): jnp.dot(lax.all_to_all(grouped, 'head', split_axis=0, concat_axis=2, tile...  5.46 us
    dot_general x1, matrix products, per_device(): jnp.einsum('bhqk,bkhe->bqhe', local_scores, v_blocks.astype(jnp.float32),...  5.17 us
  transfers between devices with their start and end apart: 7, of which 3 were waited for; matrix products, arithmetic and copies ran while one was open for 17% of the time, Pallas kernels for 0%

commit v1 on v0

--- a/solution.py
+++ b/solution.py
@@ -1,12 +1,327 @@
+import functools
 import math
 
 import jax
 import jax.numpy as jnp
 from jax import lax
+from jax.experimental import pallas as pl
+from jax.experimental.pallas import tpu as pltpu
 from jax.sharding import PartitionSpec as P
 
 HD = 128
 WINDOW = 2048
+MESH = pl.DeviceIdType.MESH
+F32 = jnp.float32
+BF16 = jnp.bfloat16
+RATE = math.log2(math.e) / math.sqrt(HD)
+FLOOR = -1e30
+
+
+def dot_nt(a, b):
+    return lax.dot_general(a, b, (((1,), (1,)), ((), ())), preferred_element_type=F32)
+
+
+def dot_tn(a, b):
+    return lax.dot_general(a, b, (((0,), (0,)), ((), ())), preferred_element_type=F32)
+
+
+def kernel(
+    peers, q_ref, k_ref, v_ref, w_hbm, out_ref,
+    w_ref, kbuf, vbuf, qbuf, o_send, o_recv, t_send, t_recv, s_send, s_recv, acc, lin, stat,
+    mixed, gathered, w_sem, kv_tx, kv_rx, q_tx, q_rx, o_tx, o_rx, t_tx, t_rx, s_tx, s_rx, m_tx, m_rx,
+):
+    seq = lax.axis_index("seq")
+    here = lax.axis_index("head")
+    blocks = lax.axis_size("seq")
+    length, width = q_ref.shape
+    heads = width // HD
+    share = length // peers
+
+    load_w = pltpu.make_async_copy(w_hbm, w_ref, w_sem)
+    load_w.start()
+
+    barrier = pltpu.get_barrier_semaphore()
+    for step in range(1, blocks):
+        pl.semaphore_signal(
+            barrier, inc=1, device_id={"seq": lax.rem(seq + step, blocks)}, device_id_type=MESH
+        )
+    for step in range(1, peers):
+        pl.semaphore_signal(
+            barrier, inc=1, device_id={"head": lax.rem(here + step, peers)}, device_id_type=MESH
+        )
+    pl.semaphore_wait(barrier, blocks - 1 + peers - 1)
+
+    def cols(h):
+        return pl.ds(pl.multiple_of(h * HD, HD), HD)
+
+    def remote(source, target, tx, rx, device):
+        return pltpu.make_async_remote_copy(
+            src_ref=source, dst_ref=target, send_sem=tx, recv_sem=rx,
+            device_id=device, device_id_type=MESH,
+        )
+
+    def key_copy(h):
+        return remote(
+            k_ref.at[:, cols(h)], kbuf.at[:, cols(h)], kv_tx.at[0, h], kv_rx.at[0, h], {"seq": 1}
+        )
+
+    def value_copy(h):
+        return remote(
+            v_ref.at[:, cols(h)], vbuf.at[:, cols(h)], kv_tx.at[1, h], kv_rx.at[1, h], {"seq": 1}
+        )
+
+    def query_copy(h, slot, target):
+        return remote(
+            q_ref.at[:, cols(h)], qbuf.at[slot, :, cols(h)],
+            q_tx.at[slot, h], q_rx.at[slot, h], {"seq": target},
+        )
+
+    def relay_copy(h):
+        return remote(
+            qbuf.at[1, :, cols(h)], qbuf.at[1, :, cols(h)], q_tx.at[1, h], q_rx.at[1, h], {"seq": 1}
+        )
+
+    def part_copies(h, out_slot, in_slot, target):
+        return (
+            remote(
+                t_send.at[out_slot, h], t_recv.at[in_slot, h],
+                t_tx.at[out_slot, h], t_rx.at[in_slot, h], {"seq": target},
+            ),
+            remote(
+                o_send.at[out_slot, h], o_recv.at[in_slot, h],
+                o_tx.at[out_slot, h], o_rx.at[in_slot, h], {"seq": target},
+            ),
+        )
+
+    def state_copy(h, tx_slot, in_slot, target):
+        return remote(
+            s_send.at[h], s_recv.at[in_slot, h], s_tx.at[tx_slot, h], s_rx.at[in_slot, h],
+            {"seq": target},
+        )
+
+    def mixed_copy(h, step):
+        target = lax.rem(here + step, peers)
+        return remote(
+            mixed.at[pl.ds(pl.multiple_of(h * HD, HD), HD), pl.ds(pl.multiple_of(target * share, HD), share)],
+            gathered.at[pl.ds(pl.multiple_of(here * width + h * HD, HD), HD), :],
+            m_tx.at[h, step], m_rx.at[h, step], {"head": target},
+        )
+
+    def loop(body):
+        lax.fori_loop(0, heads, lambda h, c: (body(h), c)[1], 0)
+
+    causal = lax.broadcasted_iota(jnp.int32, (length, length), 0) <= lax.broadcasted_iota(
+        jnp.int32, (length, length), 1
+    )
+
+    def own(h):
+        query, key, value = q_ref[:, cols(h)], k_ref[:, cols(h)], v_ref[:, cols(h)]
+        scores = dot_nt(key, query)
+        lin[h] = dot_tn(value, jnp.where(causal, scores, 0.0).astype(BF16))
+        scores = jnp.where(causal, scores, FLOOR)
+        top = jnp.max(scores, axis=0, keepdims=True)
+        expo = jnp.exp2((scores - top) * RATE)
+        stat[h, 0:1, :] = top
+        stat[h, 1:2, :] = jnp.sum(expo, axis=0, keepdims=True)
+        acc[h] = dot_tn(value, expo.astype(BF16))
+
+    def part(query, pairs):
+        scores = [dot_nt(key, query) for key, _ in pairs]
+        top = functools.reduce(jnp.maximum, [jnp.max(s, axis=0, keepdims=True) for s in scores])
+        expo = [jnp.exp2((s - top) * RATE) for s in scores]
+        total = sum(jnp.sum(e, axis=0, keepdims=True) for e in expo)
+        summed = sum(dot_tn(value, e.astype(BF16)) for e, (_, value) in zip(expo, pairs))
+        return top, total, summed
+
+    def emit(h, slot, top, total, summed):
+        row = lax.broadcasted_iota(jnp.int32, t_send.shape[2:], 0)
+        t_send[slot, h] = jnp.where(row == 0, top, total)
+        o_send[slot, h] = (summed / total).astype(BF16)
+
+    def merged(h, others):
+        tops = [stat[h, 0:1, :]] + [o[0] for o in others]
+        top = functools.reduce(jnp.maximum, tops)
+        scale = jnp.exp2((tops[0] - top) * RATE)
+        total = scale * stat[h, 1:2, :]
+        summed = scale * acc[h]
+        for other_top, other_total, other, normal in others:
+            scale = jnp.exp2((other_top - top) * RATE)
+            total += scale * other_total
+            summed += (scale * other_total if normal else scale) * other
+        return summed / total
+
+    def received(h, slot):
+        return t_recv[slot, h, 0:1, :], t_recv[slot, h, 1:2, :], o_recv[slot, h].astype(F32), True
+
+    def finish(h, windowed, linear):
+        square = jnp.mean(linear * linear, axis=0, keepdims=True)
+        rows = pl.ds(pl.multiple_of(h * HD, HD), HD)
+        mixed[rows, :] = (linear / jnp.sqrt(square + 1e-06) + windowed).astype(BF16)
+        for step in range(1, peers):
+            mixed_copy(h, step).start()
+        gathered[pl.ds(pl.multiple_of(here * width + h * HD, HD), HD), :] = mixed[
+            rows, pl.ds(pl.multiple_of(here * share, HD), share)
+        ]
+
+    @pl.when(seq == 0)
+    def _():
+        def send(h):
+            key_copy(h).start()
+            value_copy(h).start()
+
+        def work(h):
+            own(h)
+            finish(h, acc[h] / stat[h, 1:2, :], lin[h])
+
+        def drain(h):
+            key_copy(h).wait_send()
+            value_copy(h).wait_send()
+
+        loop(send)
+        loop(work)
+        loop(drain)
+
+    @pl.when(seq == 1)
+    def _():
+        def work(h):
+            key_copy(h).wait_recv()
+            value_copy(h).wait_recv()
+            first = (kbuf[:, cols(h)], vbuf[:, cols(h)])
+            second = (k_ref[:, cols(h)], v_ref[:, cols(h)])
+            early = dot_tn(first[1], first[0])
+            s_send[h] = (early + dot_tn(second[1], second[0])).astype(BF16)
+            state_copy(h, 0, 0, 2).start()
+            state_copy(h, 1, 0, 3).start()
+            query_copy(h, 0, 1).wait_recv()
+            emit(h, 0, *part(qbuf[0, :, cols(h)], (first, second)))
+            for copy in part_copies(h, 0, 0, 2):
+                copy.start()
+            query = q_ref[:, cols(h)]
+            windowed = merged(h, [part(query, (first,)) + (False,)])
+            finish(h, windowed, lin[h] + dot_nt(early.astype(BF16), query))
+            relay_copy(h).wait_recv()
+            emit(h, 1, *part(qbuf[1, :, cols(h)], (first, second)))
+            for copy in part_copies(h, 1, 0, 3):
+                copy.start()
+
+        def drain(h):
+            state_copy(h, 0, 0, 2).wait_send()
+            state_copy(h, 1, 0, 3).wait_send()
+            for copy in part_copies(h, 0, 0, 2) + part_copies(h, 1, 0, 3):
+                copy.wait_send()
+
+        loop(own)
+        loop(work)
+        loop(drain)
+
+    @pl.when(seq == 2)
+    def _():
+        def first(h):
+            query_copy(h, 0, 1).start()
+            own(h)
+            key, value = k_ref[:, cols(h)], v_ref[:, cols(h)]
+            s_send[h] = dot_tn(value, key).astype(BF16)
+            state_copy(h, 0, 1, 3).start()
+            query_copy(h, 1, 2).wait_recv()
+            relay_copy(h).start()
+            emit(h, 1, *part(qbuf[1, :, cols(h)], ((key, value),)))
+            for copy in part_copies(h, 1, 1, 3):
+                copy.start()
+
+        def second(h):
+            state_copy(h, 0, 0, 2).wait_recv()
+            for copy in part_copies(h, 0, 0, 2):
+                copy.wait_recv()
+            linear = lin[h] + dot_nt(s_recv[0, h], q_ref[:, cols(h)])
+            finish(h, merged(h, [received(h, 0)]), linear)
+
+        def drain(h):
+            query_copy(h, 0, 1).wait_send()
+            relay_copy(h).wait_send()
+            state_copy(h, 0, 1, 3).wait_send()
+            for copy in part_copies(h, 1, 1, 3):
+                copy.wait_send()
+
+        loop(first)
+        loop(second)
+        loop(drain)
+
+    @pl.when(seq == 3)
+    def _():
+        def send(h):
+            query_copy(h, 1, 2).start()
+
+        def work(h):
+            state_copy(h, 0, 1, 3).wait_recv()
+            state_copy(h, 1, 0, 3).wait_recv()
+            for copy in part_copies(h, 1, 1, 3) + part_copies(h, 1, 0, 3):
+                copy.wait_recv()
+            query = q_ref[:, cols(h)]
+            linear = lin[h] + dot_nt(s_recv[0, h], query) + dot_nt(s_recv[1, h], query)
+            finish(h, merged(h, [received(h, 0), received(h, 1)]), linear)
+
+        def drain(h):
+            query_copy(h, 1, 2).wait_send()
+
+        loop(send)
+        loop(own)
+        loop(work)
+        loop(drain)
+
+    load_w.wait()
+
+    def collect(h):
+        for step in range(1, peers):
+            mixed_copy(h, step).wait()
+
+    loop(collect)
+    tile = math.gcd(w_ref.shape[1], 512)
+    left = gathered[...].T
+
+    @pl.loop(0, w_ref.shape[1] // tile)
+    def _(index):
+        part_cols = pl.ds(pl.multiple_of(index * tile, tile), tile)
+        out_ref[:, part_cols] = jnp.dot(
+            left, w_ref[:, part_cols], preferred_element_type=F32
+        ).astype(BF16)
+
+
+def fused(queries, keys, values, w_out):
+    peers = lax.axis_size("head")
+    length, width = queries.shape
+    heads = width // HD
+    share = length // peers
+    dma = pltpu.SemaphoreType.DMA
+    vmem = pl.BlockSpec(memory_space=pltpu.VMEM)
+    return pl.pallas_call(
+        functools.partial(kernel, peers),
+        out_shape=jax.ShapeDtypeStruct((share, w_out.shape[1]), BF16),
+        in_specs=[vmem, vmem, vmem, pl.BlockSpec(memory_space=pl.ANY)],
+        out_specs=vmem,
+        scratch_shapes=[
+            pltpu.VMEM(w_out.shape, BF16),
+            pltpu.VMEM((length, width), BF16),
+            pltpu.VMEM((length, width), BF16),
+            pltpu.VMEM((2, length, width), BF16),
+            pltpu.VMEM((2, heads, HD, length), BF16),
+            pltpu.VMEM((2, heads, HD, length), BF16),
+            pltpu.VMEM((2, heads, 8, length), F32),
+            pltpu.VMEM((2, heads, 8, length), F32),
+            pltpu.VMEM((heads, HD, HD), BF16),
+            pltpu.VMEM((2, heads, HD, HD), BF16),
+            pltpu.VMEM((heads, HD, length), F32),
+            pltpu.VMEM((heads, HD, length), F32),
+            pltpu.VMEM((heads, 8, length), F32),
+            pltpu.VMEM((width, length), BF16),
+            pltpu.VMEM((peers * width, share), BF16),
+            dma, dma((2, heads)), dma((2, heads)), dma((2, heads)), dma((2, heads)),
+            dma((2, heads)), dma((2, heads)), dma((2, heads)), dma((2, heads)),
+            dma((2, heads)), dma((2, heads)), dma((heads, peers)), dma((heads, peers)),
+        ],
+        compiler_params=pltpu.CompilerParams(
+            collective_id=0, has_side_effects=True, vmem_limit_bytes=56 * 1024 * 1024
+        ),
+    )(queries, keys, values, w_out)
 
 
 def shifted(value, axis, steps):
@@ -15,7 +330,16 @@
     return lax.ppermute(value, axis, [(source, source + steps) for source in range(first, last)])
 
 
+def fits(queries):
+    length, width = queries.shape
+    blocks = lax.axis_size("seq")
+    share = length // lax.axis_size("head")
+    return blocks == 4 and blocks * length <= WINDOW and share % HD == 0 and width % HD == 0
+
+
 def per_device(queries, keys, values, w_out):
+    if fits(queries):
+        return fused(queries, keys, values, w_out)
     length_dev, width = queries.shape
     heads_dev = width // HD
     block_rows = min(512, length_dev)

time: 175 us -> 53.3 us (0.30)
  the two profiles are of different devices: /device:TPU:16 before, /device:TPU:25 now
where the time goes in v1:
time: 53.3 us; the launch traced here: 53.1 us
  Pallas kernels  51.3 us (96%)
  local copies, waits for them, and re-layouts  1.88 us (4%)
    pallas_call x1, Pallas kernels, fused(): pl.pallas_call(functools.partial(kernel, peers), out_shape=jax.ShapeDtype...  51.3 us
    unnamed x1, local copies, waits for them, and re-layouts  1.88 us

profile of v1, /device:TPU:25, one launch (start us, length us, event | category | flops | bytes accessed | tf_op | source)
XLA Modules:
  0.0 53.1 jit_solution(13342811955902442174)
XLA Ops:
  0.0 51.3 %shard_map.46 = bf16[128,2048]{1,0:T(8,128)(2,1)} custom-call(bf16[512,512]{1,0:T(8,128)(2,1)} %q_ref.1, bf16[512,512]{1,0:T(8,128)(2,1)} %k_ref.1, bf16[512,512]{1,0:T(8,128)(2,1)} %v_ref.1, bf16[2048,2048]{1,0:T(8,128)(2,1)} %w_hbm.1), custom_call_target="tpu_custom_call" | custom-call | tf_op jit(solution)/shard_map/pallas_call | solution.py:296
  51.3 1.9 %copy.6 = bf16[128,2048]{1,0:T(8,128)(2,1)} copy(bf16[128,2048]{1,0:T(8,128)(2,1)} %shard_map.46) | data formatting | bytes 1048576

commit v2 on v1

--- a/solution.py
+++ b/solution.py
@@ -27,7 +27,7 @@
 
 def kernel(
     peers, q_ref, k_ref, v_ref, w_hbm, out_ref,
-    w_ref, kbuf, vbuf, qbuf, o_send, o_recv, t_send, t_recv, s_send, s_recv, acc, lin, stat,
+    w_ref, summed, kbuf, vbuf, qbuf, o_send, o_recv, t_send, t_recv, s_send, s_recv, acc, lin, stat,
     mixed, gathered, w_sem, kv_tx, kv_rx, q_tx, q_rx, o_tx, o_rx, t_tx, t_rx, s_tx, s_rx, m_tx, m_rx,
 ):
     seq = lax.axis_index("seq")
@@ -37,8 +37,18 @@
     heads = width // HD
     share = length // peers
 
-    load_w = pltpu.make_async_copy(w_hbm, w_ref, w_sem)
-    load_w.start()
+    def load_w(h, peer):
+        return pltpu.make_async_copy(
+            w_hbm.at[pl.ds(pl.multiple_of(peer * width + h * HD, HD), HD), :],
+            w_ref.at[h, pl.ds(peer * HD, HD), :],
+            w_sem.at[h, peer],
+        )
+
+    def load_head(h):
+        for peer in range(peers):
+            load_w(h, peer).start()
+
+    lax.fori_loop(0, heads, lambda h, c: (load_head(h), c)[1], 0)
 
     barrier = pltpu.get_barrier_semaphore()
     for step in range(1, blocks):
@@ -99,11 +109,16 @@
             {"seq": target},
         )
 
+    def prefix_copy(h):
+        return remote(
+            s_recv.at[0, h], s_recv.at[0, h], s_tx.at[1, h], s_rx.at[0, h], {"seq": 3}
+        )
+
     def mixed_copy(h, step):
         target = lax.rem(here + step, peers)
         return remote(
             mixed.at[pl.ds(pl.multiple_of(h * HD, HD), HD), pl.ds(pl.multiple_of(target * share, HD), share)],
-            gathered.at[pl.ds(pl.multiple_of(here * width + h * HD, HD), HD), :],
+            gathered.at[h, pl.ds(pl.multiple_of(here * HD, HD), HD), :],
             m_tx.at[h, step], m_rx.at[h, step], {"head": target},
         )
 
@@ -117,7 +132,10 @@
     def own(h):
         query, key, value = q_ref[:, cols(h)], k_ref[:, cols(h)], v_ref[:, cols(h)]
         scores = dot_nt(key, query)
-        lin[h] = dot_tn(value, jnp.where(causal, scores, 0.0).astype(BF16))
+        kept = jnp.where(causal, scores, 0.0)
+        coarse = kept.astype(BF16)
+        fine = (kept - coarse.astype(F32)).astype(BF16)
+        lin[h] = dot_tn(value, coarse) + dot_tn(value, fine)
         scores = jnp.where(causal, scores, FLOOR)
         top = jnp.max(scores, axis=0, keepdims=True)
         expo = jnp.exp2((scores - top) * RATE)
@@ -130,25 +148,25 @@
         top = functools.reduce(jnp.maximum, [jnp.max(s, axis=0, keepdims=True) for s in scores])
         expo = [jnp.exp2((s - top) * RATE) for s in scores]
         total = sum(jnp.sum(e, axis=0, keepdims=True) for e in expo)
-        summed = sum(dot_tn(value, e.astype(BF16)) for e, (_, value) in zip(expo, pairs))
-        return top, total, summed
-
-    def emit(h, slot, top, total, summed):
+        output = sum(dot_tn(value, e.astype(BF16)) for e, (_, value) in zip(expo, pairs))
+        return top, total, output
+
+    def emit(h, slot, top, total, output):
         row = lax.broadcasted_iota(jnp.int32, t_send.shape[2:], 0)
         t_send[slot, h] = jnp.where(row == 0, top, total)
-        o_send[slot, h] = (summed / total).astype(BF16)
+        o_send[slot, h] = (output / total).astype(BF16)
 
     def merged(h, others):
         tops = [stat[h, 0:1, :]] + [o[0] for o in others]
         top = functools.reduce(jnp.maximum, tops)
         scale = jnp.exp2((tops[0] - top) * RATE)
         total = scale * stat[h, 1:2, :]
-        summed = scale * acc[h]
+        output = scale * acc[h]
         for other_top, other_total, other, normal in others:
             scale = jnp.exp2((other_top - top) * RATE)
             total += scale * other_total
-            summed += (scale * other_total if normal else scale) * other
-        return summed / total
+            output += (scale * other_total if normal else scale) * other
+        return output / total
 
     def received(h, slot):
         return t_recv[slot, h, 0:1, :], t_recv[slot, h, 1:2, :], o_recv[slot, h].astype(F32), True
@@ -159,9 +177,32 @@
         mixed[rows, :] = (linear / jnp.sqrt(square + 1e-06) + windowed).astype(BF16)
         for step in range(1, peers):
             mixed_copy(h, step).start()
-        gathered[pl.ds(pl.multiple_of(here * width + h * HD, HD), HD), :] = mixed[
+        gathered[h, pl.ds(pl.multiple_of(here * HD, HD), HD), :] = mixed[
             rows, pl.ds(pl.multiple_of(here * share, HD), share)
         ]
+
+    tile = math.gcd(w_ref.shape[2], 512)
+
+    def project(h):
+        for peer in range(peers):
+            load_w(h, peer).wait()
+        for step in range(1, peers):
+            mixed_copy(h, step).wait()
+        left = gathered[h].T
+
+        @pl.loop(0, w_ref.shape[2] // tile)
+        def _(index):
+            part_cols = pl.ds(pl.multiple_of(index * tile, tile), tile)
+            summed[:, part_cols] += jnp.dot(
+                left, w_ref[h, :, part_cols], preferred_element_type=F32
+            )
+
+    def project_before(h):
+        @pl.when(h > 0)
+        def _():
+            project(h - 1)
+
+    summed[...] = jnp.zeros_like(summed)
 
     @pl.when(seq == 0)
     def _():
@@ -172,6 +213,7 @@
         def work(h):
             own(h)
             finish(h, acc[h] / stat[h, 1:2, :], lin[h])
+            project_before(h)
 
         def drain(h):
             key_copy(h).wait_send()
@@ -184,6 +226,7 @@
     @pl.when(seq == 1)
     def _():
         def work(h):
+            project_before(h)
             key_copy(h).wait_recv()
             value_copy(h).wait_recv()
             first = (kbuf[:, cols(h)], vbuf[:, cols(h)])
@@ -191,7 +234,6 @@
             early = dot_tn(first[1], first[0])
             s_send[h] = (early + dot_tn(second[1], second[0])).astype(BF16)
             state_copy(h, 0, 0, 2).start()
-            state_copy(h, 1, 0, 3).start()
             query_copy(h, 0, 1).wait_recv()
             emit(h, 0, *part(qbuf[0, :, cols(h)], (first, second)))
             for copy in part_copies(h, 0, 0, 2):
@@ -206,7 +248,6 @@
 
         def drain(h):
             state_copy(h, 0, 0, 2).wait_send()
-            state_copy(h, 1, 0, 3).wait_send()
             for copy in part_copies(h, 0, 0, 2) + part_copies(h, 1, 0, 3):
                 copy.wait_send()
 
@@ -229,7 +270,9 @@
                 copy.start()
 
         def second(h):
+            project_before(h)
             state_copy(h, 0, 0, 2).wait_recv()
+            prefix_copy(h).start()
             for copy in part_copies(h, 0, 0, 2):
                 copy.wait_recv()
             linear = lin[h] + dot_nt(s_recv[0, h], q_ref[:, cols(h)])
@@ -239,6 +282,7 @@
             query_copy(h, 0, 1).wait_send()
             relay_copy(h).wait_send()
             state_copy(h, 0, 1, 3).wait_send()
+            prefix_copy(h).wait_send()
             for copy in part_copies(h, 1, 1, 3):
                 copy.wait_send()
 
@@ -252,8 +296,9 @@
             query_copy(h, 1, 2).start()
 
         def work(h):
+            project_before(h)
             state_copy(h, 0, 1, 3).wait_recv()
-            state_copy(h, 1, 0, 3).wait_recv()
+            prefix_copy(h).wait_recv()
             for copy in part_copies(h, 1, 1, 3) + part_copies(h, 1, 0, 3):
                 copy.wait_recv()
             query = q_ref[:, cols(h)]
@@ -268,22 +313,8 @@
         loop(work)
         loop(drain)
 
-    load_w.wait()
-
-    def collect(h):
-        for step in range(1, peers):
-            mixed_copy(h, step).wait()
-
-    loop(collect)
-    tile = math.gcd(w_ref.shape[1], 512)
-    left = gathered[...].T
-
-    @pl.loop(0, w_ref.shape[1] // tile)
-    def _(index):
-        part_cols = pl.ds(pl.multiple_of(index * tile, tile), tile)
-        out_ref[:, part_cols] = jnp.dot(
-            left, w_ref[:, part_cols], preferred_element_type=F32
-        ).astype(BF16)
+    project(heads - 1)
+    out_ref[...] = summed[...].astype(BF16)
 
 
 def fused(queries, keys, values, w_out):
@@ -296,30 +327,31 @@
     return pl.pallas_call(
         functools.partial(kernel, peers),
         out_shape=jax.ShapeDtypeStruct((share, w_out.shape[1]), BF16),
-        in_specs=[vmem, vmem, vmem, pl.BlockSpec(memory_space=pl.ANY)],
+        in_specs=[vmem, vmem, vmem, pl.BlockSpec(memory_space=pltpu.HBM)],
         out_specs=vmem,
         scratch_shapes=[
-            pltpu.VMEM(w_out.shape, BF16),
+            pltpu.VMEM((heads, peers * HD, w_out.shape[1]), BF16),
+            pltpu.VMEM((share, w_out.shape[1]), F32),
             pltpu.VMEM((length, width), BF16),
             pltpu.VMEM((length, width), BF16),
             pltpu.VMEM((2, length, width), BF16),
             pltpu.VMEM((2, heads, HD, length), BF16),
             pltpu.VMEM((2, heads, HD, length), BF16),
-            pltpu.VMEM((2, heads, 8, length), F32),
-            pltpu.VMEM((2, heads, 8, length), F32),
+            pltpu.VMEM((2, heads, 2, length), F32),
+            pltpu.VMEM((2, heads, 2, length), F32),
             pltpu.VMEM((heads, HD, HD), BF16),
             pltpu.VMEM((2, heads, HD, HD), BF16),
             pltpu.VMEM((heads, HD, length), F32),
             pltpu.VMEM((heads, HD, length), F32),
             pltpu.VMEM((heads, 8, length), F32),
             pltpu.VMEM((width, length), BF16),
-            pltpu.VMEM((peers * width, share), BF16),
-            dma, dma((2, heads)), dma((2, heads)), dma((2, heads)), dma((2, heads)),
+            pltpu.VMEM((heads, peers * HD, share), BF16),
+            dma((heads, peers)), dma((2, heads)), dma((2, heads)), dma((2, heads)), dma((2, heads)),
             dma((2, heads)), dma((2, heads)), dma((2, heads)), dma((2, heads)),
             dma((2, heads)), dma((2, heads)), dma((heads, peers)), dma((heads, peers)),
         ],
         compiler_params=pltpu.CompilerParams(
-            collective_id=0, has_side_effects=True, vmem_limit_bytes=56 * 1024 * 1024
+            collective_id=0, has_side_effects=True, vmem_limit_bytes=48 * 1024 * 1024
         ),
     )(queries, keys, values, w_out)
 

time: 53.3 us -> 53.1 us (level)
  Pallas kernels: 51.3 us -> 48.9 us
  local copies, waits for them, and re-layouts: 1.88 us -> 3.92 us
    pallas_call x1, Pallas kernels: 51.3 us -> 48.9 us  [fused(): pl.pallas_call(functools.partial(kernel, peers), out_shape=jax.ShapeDtype...]
    unnamed x1 -> x7, local copies, waits for them, and re-layouts: 1.88 us -> 3.92 us
where the time goes in v2:
time: 53.1 us; the launch traced here: 52.8 us
  Pallas kernels  48.9 us (92%)
  local copies, waits for them, and re-layouts  3.92 us (7%)
    pallas_call x1, Pallas kernels, fused(): pl.pallas_call(functools.partial(kernel, peers), out_shape=jax.ShapeDtype...  48.9 us
    unnamed x7, local copies, waits for them, and re-layouts  3.92 us

profile of v2, /device:TPU:25, one launch (start us, length us, event | category | flops | bytes accessed | tf_op | source)
XLA Modules:
  0.0 52.8 jit_solution(18415071703613642599)
XLA Ops:
  0.0 0.0 copy-start
  0.0 1.0 %copy-done = bf16[512,512]{1,0:T(8,128)(2,1)S(1)} copy-done((bf16[512,512]{1,0:T(8,128)(2,1)S(1)}, bf16[512,512]{1,0:T(8,128)(2,1)}, u32[]{:S(2)}) %copy-start) | copy-done | bytes 524312
  1.0 0.0 copy-start.1
  1.0 1.0 %copy-done.1 = bf16[512,512]{1,0:T(8,128)(2,1)S(1)} copy-done((bf16[512,512]{1,0:T(8,128)(2,1)S(1)}, bf16[512,512]{1,0:T(8,128)(2,1)}, u32[]{:S(2)}) %copy-start.1) | copy-done | bytes 524312
  2.1 0.0 copy-start.2
  2.1 1.0 %copy-done.2 = bf16[512,512]{1,0:T(8,128)(2,1)S(1)} copy-done((bf16[512,512]{1,0:T(8,128)(2,1)S(1)}, bf16[512,512]{1,0:T(8,128)(2,1)}, u32[]{:S(2)}) %copy-start.2) | copy-done | bytes 524312
  3.1 48.9 %shard_map.46 = bf16[128,2048]{1,0:T(8,128)(2,1)S(1)} custom-call(bf16[512,512]{1,0:T(8,128)(2,1)S(1)} %copy-done, bf16[512,512]{1,0:T(8,128)(2,1)S(1)} %copy-done.1, bf16[512,512]{1,0:T(8,128)(2,1)S(1)} %copy-done.2, bf16[2048,2048]{1,0:T(8,128)(2,1)} %w_hbm.1), custom_call_target="tpu_custom_call" | custom-call | tf_op jit(solution)/shard_map/pallas_call | solution.py:327
  52.0 0.8 %copy.6 = bf16[128,2048]{1,0:T(8,128)(2,1)} copy(bf16[128,2048]{1,0:T(8,128)(2,1)S(1)} %shard_map.46) | data formatting | bytes 1048576
Async XLA Ops:
  0.0 1.0 %copy-start = (bf16[512,512]{1,0:T(8,128)(2,1)S(1)}, bf16[512,512]{1,0:T(8,128)(2,1)}, u32[]{:S(2)}) copy-start(bf16[512,512]{1,0:T(8,128)(2,1)} %q_ref.1) | copy-start | bytes 1572868
  1.0 1.0 %copy-start.1 = (bf16[512,512]{1,0:T(8,128)(2,1)S(1)}, bf16[512,512]{1,0:T(8,128)(2,1)}, u32[]{:S(2)}) copy-start(bf16[512,512]{1,0:T(8,128)(2,1)} %k_ref.1) | copy-start | bytes 1572868
  2.1 1.0 %copy-start.2 = (bf16[512,512]{1,0:T(8,128)(2,1)S(1)}, bf16[512,512]{1,0:T(8,128)(2,1)}, u32[]{:S(2)}) copy-start(bf16[512,512]{1,0:T(8,128)(2,1)} %v_ref.1) | copy-start | bytes 1572868

commit v3 on v2

--- a/solution.py
+++ b/solution.py
@@ -26,9 +26,9 @@
 
 
 def kernel(
-    peers, q_ref, k_ref, v_ref, w_hbm, out_ref,
+    peers, q_hbm, k_hbm, v_hbm, w_hbm, out_ref, q_ref, k_ref, v_ref,
     w_ref, summed, kbuf, vbuf, qbuf, o_send, o_recv, t_send, t_recv, s_send, s_recv, acc, lin, stat,
-    mixed, gathered, w_sem, kv_tx, kv_rx, q_tx, q_rx, o_tx, o_rx, t_tx, t_rx, s_tx, s_rx, m_tx, m_rx,
+    mixed, gathered, in_sem, w_sem, kv_tx, kv_rx, q_tx, q_rx, o_tx, o_rx, t_tx, t_rx, s_tx, s_rx, m_tx, m_rx,
 ):
     seq = lax.axis_index("seq")
     here = lax.axis_index("head")
@@ -37,6 +37,13 @@
     heads = width // HD
     share = length // peers
 
+    loads = [
+        pltpu.make_async_copy(source, target, in_sem.at[i])
+        for i, (source, target) in enumerate(((q_hbm, q_ref), (k_hbm, k_ref), (v_hbm, v_ref)))
+    ]
+    for load in loads:
+        load.start()
+
     def load_w(h, peer):
         return pltpu.make_async_copy(
             w_hbm.at[pl.ds(pl.multiple_of(peer * width + h * HD, HD), HD), :],
@@ -48,7 +55,6 @@
         for peer in range(peers):
             load_w(h, peer).start()
 
-    lax.fori_loop(0, heads, lambda h, c: (load_head(h), c)[1], 0)
 
     barrier = pltpu.get_barrier_semaphore()
     for step in range(1, blocks):
@@ -60,6 +66,9 @@
             barrier, inc=1, device_id={"head": lax.rem(here + step, peers)}, device_id_type=MESH
         )
     pl.semaphore_wait(barrier, blocks - 1 + peers - 1)
+    for load in loads:
+        load.wait()
+    lax.fori_loop(0, heads, lambda h, c: (load_head(h), c)[1], 0)
 
     def cols(h):
         return pl.ds(pl.multiple_of(h * HD, HD), HD)
@@ -234,6 +243,10 @@
             early = dot_tn(first[1], first[0])
             s_send[h] = (early + dot_tn(second[1], second[0])).astype(BF16)
             state_copy(h, 0, 0, 2).start()
+            relay_copy(h).wait_recv()
+            emit(h, 1, *part(qbuf[1, :, cols(h)], (first, second)))
+            for copy in part_copies(h, 1, 0, 3):
+                copy.start()
             query_copy(h, 0, 1).wait_recv()
             emit(h, 0, *part(qbuf[0, :, cols(h)], (first, second)))
             for copy in part_copies(h, 0, 0, 2):
@@ -241,10 +254,6 @@
             query = q_ref[:, cols(h)]
             windowed = merged(h, [part(query, (first,)) + (False,)])
             finish(h, windowed, lin[h] + dot_nt(early.astype(BF16), query))
-            relay_copy(h).wait_recv()
-            emit(h, 1, *part(qbuf[1, :, cols(h)], (first, second)))
-            for copy in part_copies(h, 1, 0, 3):
-                copy.start()
 
         def drain(h):
             state_copy(h, 0, 0, 2).wait_send()
@@ -327,9 +336,12 @@
     return pl.pallas_call(
         functools.partial(kernel, peers),
         out_shape=jax.ShapeDtypeStruct((share, w_out.shape[1]), BF16),
-        in_specs=[vmem, vmem, vmem, pl.BlockSpec(memory_space=pltpu.HBM)],
+        in_specs=[pl.BlockSpec(memory_space=pltpu.HBM)] * 4,
         out_specs=vmem,
         scratch_shapes=[
+            pltpu.VMEM((length, width), BF16),
+            pltpu.VMEM((length, width), BF16),
+            pltpu.VMEM((length, width), BF16),
             pltpu.VMEM((heads, peers * HD, w_out.shape[1]), BF16),
             pltpu.VMEM((share, w_out.shape[1]), F32),
             pltpu.VMEM((length, width), BF16),
@@ -346,7 +358,7 @@
             pltpu.VMEM((heads, 8, length), F32),
             pltpu.VMEM((width, length), BF16),
             pltpu.VMEM((heads, peers * HD, share), BF16),
-            dma((heads, peers)), dma((2, heads)), dma((2, heads)), dma((2, heads)), dma((2, heads)),
+            dma((3,)), dma((heads, peers)), dma((2, heads)), dma((2, heads)), dma((2, heads)), dma((2, heads)),
             dma((2, heads)), dma((2, heads)), dma((2, heads)), dma((2, heads)),
             dma((2, heads)), dma((2, heads)), dma((heads, peers)), dma((heads, peers)),
         ],

time: 53.1 us -> 54.3 us (1.023); the launches traced: 52.8 us -> 53.4 us
  Pallas kernels: 48.9 us -> 49.5 us
    pallas_call x1, Pallas kernels: 48.9 us -> 49.5 us  [fused(): pl.pallas_call(functools.partial(kernel, peers), out_shape=jax.ShapeDtype...]
where the time goes in v3:
time: 54.3 us; the launch traced here: 53.4 us
  Pallas kernels  49.5 us (91%)
  local copies, waits for them, and re-layouts  3.92 us (7%)
    pallas_call x1, Pallas kernels, fused(): pl.pallas_call(functools.partial(kernel, peers), out_shape=jax.ShapeDtype...  49.5 us
    unnamed x7, local copies, waits for them, and re-layouts  3.92 us

profile of v3, /device:TPU:25, one launch (start us, length us, event | category | flops | bytes accessed | tf_op | source)
XLA Modules:
  0.0 53.4 jit_solution(6516544011308521597)
XLA Ops:
  0.0 0.0 copy-start
  0.0 1.0 %copy-done = bf16[512,512]{1,0:T(8,128)(2,1)S(1)} copy-done((bf16[512,512]{1,0:T(8,128)(2,1)S(1)}, bf16[512,512]{1,0:T(8,128)(2,1)}, u32[]{:S(2)}) %copy-start) | copy-done | bytes 524312
  1.0 0.0 copy-start.1
  1.0 1.0 %copy-done.1 = bf16[512,512]{1,0:T(8,128)(2,1)S(1)} copy-done((bf16[512,512]{1,0:T(8,128)(2,1)S(1)}, bf16[512,512]{1,0:T(8,128)(2,1)}, u32[]{:S(2)}) %copy-start.1) | copy-done | bytes 524312
  2.1 0.0 copy-start.2
  2.1 1.0 %copy-done.2 = bf16[512,512]{1,0:T(8,128)(2,1)S(1)} copy-done((bf16[512,512]{1,0:T(8,128)(2,1)S(1)}, bf16[512,512]{1,0:T(8,128)(2,1)}, u32[]{:S(2)}) %copy-start.2) | copy-done | bytes 524312
  3.1 49.5 %shard_map.46 = bf16[128,2048]{1,0:T(8,128)(2,1)S(1)} custom-call(bf16[512,512]{1,0:T(8,128)(2,1)S(1)} %copy-done, bf16[512,512]{1,0:T(8,128)(2,1)S(1)} %copy-done.1, bf16[512,512]{1,0:T(8,128)(2,1)S(1)} %copy-done.2, bf16[2048,2048]{1,0:T(8,128)(2,1)} %w_hbm.1), custom_call_target="tpu_custom_call" | custom-call | tf_op jit(solution)/shard_map/pallas_call | solution.py:336
  52.6 0.8 %copy.6 = bf16[128,2048]{1,0:T(8,128)(2,1)} copy(bf16[128,2048]{1,0:T(8,128)(2,1)S(1)} %shard_map.46) | data formatting | bytes 1048576
Async XLA Ops:
  0.0 1.0 %copy-start = (bf16[512,512]{1,0:T(8,128)(2,1)S(1)}, bf16[512,512]{1,0:T(8,128)(2,1)}, u32[]{:S(2)}) copy-start(bf16[512,512]{1,0:T(8,128)(2,1)} %q_hbm.1) | copy-start | bytes 1572868
  1.0 1.0 %copy-start.1 = (bf16[512,512]{1,0:T(8,128)(2,1)S(1)}, bf16[512,512]{1,0:T(8,128)(2,1)}, u32[]{:S(2)}) copy-start(bf16[512,512]{1,0:T(8,128)(2,1)} %k_hbm.1) | copy-start | bytes 1572868
  2.1 1.0 %copy-start.2 = (bf16[512,512]{1,0:T(8,128)(2,1)S(1)}, bf16[512,512]{1,0:T(8,128)(2,1)}, u32[]{:S(2)}) copy-start(bf16[512,512]{1,0:T(8,128)(2,1)} %v_hbm.1) | copy-start | bytes 1572868

commit v4 on v3

--- a/solution.py
+++ b/solution.py
@@ -243,10 +243,6 @@
             early = dot_tn(first[1], first[0])
             s_send[h] = (early + dot_tn(second[1], second[0])).astype(BF16)
             state_copy(h, 0, 0, 2).start()
-            relay_copy(h).wait_recv()
-            emit(h, 1, *part(qbuf[1, :, cols(h)], (first, second)))
-            for copy in part_copies(h, 1, 0, 3):
-                copy.start()
             query_copy(h, 0, 1).wait_recv()
             emit(h, 0, *part(qbuf[0, :, cols(h)], (first, second)))
             for copy in part_copies(h, 0, 0, 2):
@@ -254,6 +250,10 @@
             query = q_ref[:, cols(h)]
             windowed = merged(h, [part(query, (first,)) + (False,)])
             finish(h, windowed, lin[h] + dot_nt(early.astype(BF16), query))
+            relay_copy(h).wait_recv()
+            emit(h, 1, *part(qbuf[1, :, cols(h)], (first, second)))
+            for copy in part_copies(h, 1, 0, 3):
+                copy.start()
 
         def drain(h):
             state_copy(h, 0, 0, 2).wait_send()
@@ -363,7 +363,7 @@
             dma((2, heads)), dma((2, heads)), dma((heads, peers)), dma((heads, peers)),
         ],
         compiler_params=pltpu.CompilerParams(
-            collective_id=0, has_side_effects=True, vmem_limit_bytes=48 * 1024 * 1024
+            collective_id=0, has_side_effects=True, vmem_limit_bytes=56 * 1024 * 1024
         ),
     )(queries, keys, values, w_out)
 

time: 54.3 us -> 51.7 us (0.952); the launches traced: 53.4 us -> 51.6 us
  local copies, waits for them, and re-layouts: 3.92 us -> 1.88 us
    unnamed x7 -> x1, local copies, waits for them, and re-layouts: 3.92 us -> 1.88 us
where the time goes in v4:
time: 51.7 us; the launch traced here: 51.6 us
  Pallas kernels  49.7 us (96%)
  local copies, waits for them, and re-layouts  1.88 us (4%)
    pallas_call x1, Pallas kernels, fused(): pl.pallas_call(functools.partial(kernel, peers), out_shape=jax.ShapeDtype...  49.7 us
    unnamed x1, local copies, waits for them, and re-layouts  1.88 us

profile of v4, /device:TPU:25, one launch (start us, length us, event | category | flops | bytes accessed | tf_op | source)
XLA Modules:
  0.0 51.6 jit_solution(4858589241006081204)
XLA Ops:
  0.0 49.7 %shard_map.46 = bf16[128,2048]{1,0:T(8,128)(2,1)} custom-call(bf16[512,512]{1,0:T(8,128)(2,1)} %q_hbm.1, bf16[512,512]{1,0:T(8,128)(2,1)} %k_hbm.1, bf16[512,512]{1,0:T(8,128)(2,1)} %v_hbm.1, bf16[2048,2048]{1,0:T(8,128)(2,1)} %w_hbm.1), custom_call_target="tpu_custom_call" | custom-call | tf_op jit(solution)/shard_map/pallas_call | solution.py:336
  49.7 1.9 %copy.6 = bf16[128,2048]{1,0:T(8,128)(2,1)} copy(bf16[128,2048]{1,0:T(8,128)(2,1)} %shard_map.46) | data formatting | bytes 1048576
